TPU v7x, 32 devices: a whole 2x2x4 slice. The times are simulated.
32 devices in a mesh: seq: 16 (over z, y, x), chan: 2 (over core).
Axes of the slice: x: 2, y: 2, z: 4, core: 2. Of those that a mesh axis runs over, the one named last changes fastest.
Arguments:
- x_in: bfloat16 [32768, 2048], P('seq', 'chan'), may hold values from -6 to 6
- gate_in: bfloat16 [32768, 2048], P('seq', 'chan'), may hold values from -70 to 70
- b_in: bfloat16 [32768, 64], P('seq'), may hold values from -0.75 to 0.75
- c_in: bfloat16 [32768, 64], P('seq'), may hold values from -6 to 6
- step_size: float32 [32, 32768], P('chan', 'seq'), may hold values from 0 to 1, as said below
- log_keep: float32 [32, 32768], P('chan', 'seq'), may hold values from -2 to 0
- skip_gain: float32 [32], P('chan'), may hold values from 0.5 to 1.5
- norm_gain: float32 [2048], P('chan'), may hold values from 0.25 to 1.75
Outputs:
- mixed: bfloat16 [32768, 2048], P('seq', 'chan')
Inputs may be any that keep to these rules, and one draw needn't show every extreme that they name: `step_size`: positive.
All inputs are finite; a program needn't handle non-finite values.
Results may differ from a plain program's by a relative error of at most 0.005.
Values sent between devices are 32-bit elements; how exact they have to be, the bound alone decides.
A program may use at most 64 MiB of HBM per device.

v0:
```python
import jax
import jax.numpy as jnp
from jax import lax
from jax.sharding import PartitionSpec as P

CH = 2048
BLOCK = 256


epsilon = 1e-05


def incoming_state(device_total, end_flat):
    totals = lax.all_gather(device_total[None, :], "seq", axis=0, tiled=True)
    my_index = lax.axis_index("seq")
    device_rank = jnp.arange(totals.shape[0], dtype=jnp.int32)[:, None]
    inclusive = jnp.cumsum(totals, axis=0)
    exclusive = inclusive - totals
    own_prefix = jnp.sum(jnp.where(device_rank == my_index, exclusive, 0.0), axis=0)
    factors = jnp.where(
        device_rank < my_index, jnp.exp(jnp.minimum(own_prefix[None, :] - inclusive, 0.0)), 0.0
    )
    return jnp.einsum(
        "kh,khm->hm",
        factors,
        lax.all_gather(end_flat[None], "seq", axis=0, tiled=True),
        precision=lax.Precision.HIGHEST,
    )


def apply_state(c_blocks, cum_keep, states):
    state_high = states.astype(jnp.bfloat16)
    state_low = (states - state_high.astype(jnp.float32)).astype(jnp.bfloat16)
    projected = jnp.einsum(
        "btn,bhpn->bthp", c_blocks, state_high, preferred_element_type=jnp.float32
    )
    projected = projected + jnp.einsum(
        "btn,bhpn->bthp", c_blocks, state_low, preferred_element_type=jnp.float32
    )
    return jnp.exp(cum_keep).transpose(1, 2, 0)[:, :, :, None] * projected


def per_device(x_in, gate_in, b_in, c_in, step_size, log_keep, skip_gain, norm_gain):
    tokens, channels = x_in.shape
    head_count = step_size.shape[0]
    head_width = channels // head_count
    nstate = b_in.shape[1]
    block_count = tokens // BLOCK
    x_blocks = x_in.reshape(block_count, BLOCK, head_count, head_width)
    b_blocks = b_in.reshape(block_count, BLOCK, nstate)
    c_blocks = c_in.reshape(block_count, BLOCK, nstate)
    step_blocks = step_size.reshape(head_count, block_count, BLOCK)
    cum_keep = jnp.cumsum(log_keep.reshape(head_count, block_count, BLOCK), axis=2)
    block_total = cum_keep[:, :, -1]
    decayed_b = (
        (jnp.exp(block_total[:, :, None] - cum_keep) * step_blocks)[:, :, :, None]
        * b_blocks[None].astype(jnp.float32)
    ).astype(jnp.bfloat16)
    block_state = jnp.einsum(
        "bshp,hbsn->bhpn", x_blocks, decayed_b, preferred_element_type=jnp.float32
    )

    def carry_blocks(running, block_input):
        total_now, state_now = block_input
        return (jnp.exp(total_now)[:, None, None] * running + state_now, running)

    end_state, starts = lax.scan(
        carry_blocks,
        jnp.zeros((head_count, head_width, nstate), jnp.float32),
        (block_total.T, block_state),
    )
    device_total = jnp.sum(block_total, axis=1)
    prefix_total = jnp.cumsum(block_total, axis=1) - block_total
    end_flat = end_state.reshape(head_count, head_width * nstate)
    entering = incoming_state(device_total, end_flat).reshape(head_count, head_width, nstate)
    initial = jnp.exp(prefix_total).T[:, :, None, None] * entering[None] + starts
    scores = jnp.einsum("btn,bsn->bts", c_blocks, b_blocks, preferred_element_type=jnp.float32)
    row_index = lax.broadcasted_iota(jnp.int32, (BLOCK, BLOCK), 0)
    col_index = lax.broadcasted_iota(jnp.int32, (BLOCK, BLOCK), 1)
    causal = (row_index >= col_index)[None, None]
    log_gaps = cum_keep[:, :, :, None] - cum_keep[:, :, None, :]
    decays = jnp.where(causal, jnp.exp(jnp.where(causal, log_gaps, 0.0)), 0.0)
    weights = (scores[None] * decays * step_blocks[:, :, None, :]).astype(jnp.bfloat16)
    output = jnp.einsum(
        "hbts,bshp->bthp", weights, x_blocks, preferred_element_type=jnp.float32
    ) + apply_state(c_blocks, cum_keep, initial)
    output = output + skip_gain[None, None, :, None] * x_blocks.astype(jnp.float32)
    output = output.reshape(tokens, channels)
    gated_out = output * jax.nn.silu(gate_in.astype(jnp.float32))
    squares = jnp.sum(gated_out * gated_out, axis=1)
    summed = lax.psum(squares, "chan")
    row_factor = lax.rsqrt(summed / CH + epsilon)
    return (gated_out * row_factor[:, None] * norm_gain[None, :]).astype(jnp.bfloat16)


def solution(mesh):
    in_specs = (
        P("seq", "chan"),
        P("seq", "chan"),
        P("seq", None),
        P("seq", None),
        P("chan", "seq"),
        P("chan", "seq"),
        P("chan"),
        P("chan"),
    )
    out_specs = P("seq", "chan")
    return jax.shard_map(
        per_device, mesh=mesh, in_specs=in_specs, out_specs=out_specs, check_vma=False
    )
```

profile of v0, /device:TPU:25, one launch (start us, length us, event | category | flops | bytes accessed | tf_op | source)
XLA Modules:
  0.0 210.9 jit_solution(1977391375611540092)
XLA Ops:
  6.5 1.0 reshape.103
  7.6 9.0 %reduce-window.6 = f32[16,8,2,128]{3,1,2,0:T(8,128)S(1)} reduce-window(f32[16,8,2,128]{3,1,2,0:T(8,128)S(1)} %copy.42, f32[]{:T(128)} %constant.23.clone.1), window={size=1x1x1x128 pad=0_0x0_0x0_0x127_0}, to_apply=%region_0.0 | reduce-window | flops 4161536 | bytes 262148 | tf_op jit(solution)/shard_map/reduce-window
  17.1 0.3 slice_reduce_fusion
  17.7 1.0 copy.79
  18.8 11.6 %reshape.117 = bf16[8,256,16,64]{3,2,1,0:T(8,128)(2,1)} reshape(bf16[2048,1024]{1,0:T(8,128)(2,1)} %param.10) | data formatting | bytes 8388608 | tf_op jit(solution)/shard_map/reshape | solution.py:49
  30.4 10.4 %copy.49 = bf16[8,256,16,64]{1,3,2,0:T(8,128)(2,1)} copy(bf16[8,256,16,64]{3,2,1,0:T(8,128)(2,1)} %reshape.117) | data formatting | bytes 8388608 | tf_op jit(solution)/shard_map/reshape | solution.py:49
  41.1 5.4 %fusion.23 = f32[8,16,64,64]{2,3,1,0:T(8,128)} fusion(bf16[8,256,16,64]{1,3,2,0:T(8,128)(2,1)} %copy.49, f32[8,256,64]{1,2,0:T(8,128)S(1)} %copy.54, f32[16,8,256]{2,0,1:T(8,128)S(1)} %copy.53), kind=kOutput, calls=%fused_computation.35 | convolution fusion | flops 272629760 | bytes 6946816 | tf_op jit(solution)/shard_map/bshp,hbsn->bhpn/dot_general | solution.py:59
  46.4 18.3 %while.13 = (s32[]{:T(128)}, f32[16,64,64]{2,1,0:T(8,128)S(1)}, f32[8,16,64,64]{3,2,1,0:T(8,128)}, f32[8,16]{1,0:T(8,128)S(1)}, f32[8,16,64,64]{2,3,1,0:T(8,128)}, /*index=5*/s32[]{:T(128)}, s32[]{:T(128)}) while((s32[]{:T(128)}, f32[16,64,64]{2,1,0:T(8,128)S(1)}, f32[8,16,64,64]{3,2,1,0:T(8,128)}, f32[8,16]{1,0:T(8,128)S(1)}, ...), condition=%wide.region_7.8_spmd.clone, body=%wide.region_6.7_spmd.clone.sunk | while | flops 262147 | bytes 2622240 | solution.py:67
  46.4 0.9 bitcast_dynamic-update-slice_fusion.2
  47.3 1.1 constant_dynamic-slice_fusion.3
  48.4 0.2 copy.102
  48.7 0.9 bitcast_dynamic-update-slice_fusion.2
  49.6 1.1 constant_dynamic-slice_fusion.3
  51.1 0.8 bitcast_dynamic-update-slice_fusion.2
  51.9 1.1 constant_dynamic-slice_fusion.3
  53.3 0.8 bitcast_dynamic-update-slice_fusion.2
  54.2 1.1 constant_dynamic-slice_fusion.3
  55.6 0.9 bitcast_dynamic-update-slice_fusion.2
  56.5 1.1 constant_dynamic-slice_fusion.3
  57.9 0.9 bitcast_dynamic-update-slice_fusion.2
  58.8 1.1 constant_dynamic-slice_fusion.3
  60.2 0.8 bitcast_dynamic-update-slice_fusion.2
  61.0 1.1 constant_dynamic-slice_fusion.3
  62.5 0.8 bitcast_dynamic-update-slice_fusion.2
  63.3 1.1 constant_dynamic-slice_fusion.3
  64.8 0.9 broadcast_in_dim_reshape.2
  65.7 0.6 dynamic-slice
  66.9 0.2 dynamic-update-slice
  67.2 27.4 %all-reduce = f32[256]{0:T(256)S(1)} all-reduce(f32[256]{0:T(256)S(1)} %dynamic-update-slice), channel_id=2, replica_groups=mesh['seq'=16,'chan'=2] {'seq'}, use_global_device_ids=true, to_apply=%add | all-reduce | flops 256 | bytes 2048
  95.0 0.7 copy.50
  95.7 0.7 copy.100
  96.4 6.5 %copy.61 = bf16[2048,1024]{0,1:T(8,128)(2,1)} copy(bf16[2048,1024]{1,0:T(8,128)(2,1)} %param.11) | data formatting | bytes 8388608 | tf_op args[1]
  102.8 0.6 iota_compare_fusion
  103.5 0.5 fusion.29
  104.0 36.4 %all-gather.3.cloned.1.call-done = f32[16,16,4096]{2,1,0:T(8,128)} async-done(((f32[1,16,4096]{2,1,0:T(8,128)}), f32[16,16,4096]{2,1,0:T(8,128)}) %all-gather.3.cloned.1.call-update) | async-done | bytes 4194320 | tf_op jit(solution)/shard_map/all_gather | solution.py:26
  140.3 6.4 %fusion.16 = f32[16,1,4096]{2,1,0:T(1,128)S(1)} fusion(f32[16,16,1]{0,2,1:T(1,128)S(1)} %copy.63, f32[16,16,4096]{2,1,0:T(8,128)} %all-gather.3.cloned.1.call-done), kind=kOutput, calls=%fused_computation.27 | convolution fusion | flops 12582912 | bytes 4457472 | tf_op jit(solution)/shard_map/kh,khm->hm/dot_general | solution.py:23
  146.9 0.2 mul.114
  147.1 3.6 %fusion.24 = f32[8,16,64,256]{3,2,1,0:T(8,128)S(1)} fusion(f32[8,16,64,64]{3,2,1,0:T(8,128)} %get-tuple-element.34, f32[16,64,64]{2,1,0:T(8,128)S(1)} %mul.114, f32[8,16]{1,0:T(8,128)S(1)} %exponential_bitcast_fusion.1, bf16[8,256,64,1]{1,0,2,3:T(8,128)(2,1)S(1)} %bitcast.81), kind=kOutput, calls=%fused_computation.36 | convolution fusion | flops 271581184 | bytes 11010560 | tf_op jit(solution)/shard_map/btn,bhpn->bthp/dot_general | solution.py:37
  150.9 1.3 fusion.21
  152.2 0.8 copy-done.2
  153.0 13.3 %fusion.14 = f32[8,256,16,64]{1,3,2,0:T(8,128)} fusion(bf16[8,256,16,64]{1,3,2,0:T(8,128)(2,1)S(1)} %copy-done.2, f32[8,16,64,256]{3,2,1,0:T(8,128)S(1)} %fusion.21, f32[8,16,64,256]{3,2,1,0:T(8,128)S(1)} %fusion.24, f32[16]{0:T(128)S(1)} %copy-done.11, f32[8,256,16]{1,2,0:T(8,128)S(1)} %copy-done.7, f32[16,8,256]{2,0,1:T(8,128)S(1)} %bitcast.90, ...), kind=kOutput, calls=%fused_computation.22 | convolution fusion | flops 1136656384 | bytes 31916096 | tf_op jit(solution)/shard_map/hbts,bshp->bthp/dot_general | solution.py:84
  166.3 9.9 %copy.60 = f32[8,256,16,64]{1,0,3,2:T(8,128)S(1)} copy(f32[8,256,16,64]{1,3,2,0:T(8,128)} %fusion.14) | data formatting | bytes 16777216 | tf_op jit(solution)/shard_map/add | solution.py:87
  176.2 4.2 %copy.82 = f32[128,8,8,256]{3,1,2,0:T(8,128)S(1)} copy(f32[128,8,8,256]{3,2,1,0:T(8,128)S(1)} %bitcast.80) | data formatting | bytes 16777216
  180.4 3.2 %copy-done = f32[128,8,8,256]{3,1,2,0:T(8,128)} copy-done((f32[128,8,8,256]{3,1,2,0:T(8,128)}, f32[128,8,8,256]{3,1,2,0:T(8,128)S(1)}, u32[]{:S(2)}) %copy-start) | copy-done | bytes 8388632
  183.6 2.7 %multiply_reduce_fusion = f32[2048]{0:T(1024)S(1)} fusion(f32[2048,1024]{0,1:T(8,128)S(1)} %bitcast.78, bf16[2048,1024]{0,1:T(8,128)(2,1)S(1)} %copy-done.1), kind=kLoop, calls=%fused_computation.24 | loop fusion | flops 16775168 | bytes 12591104 | tf_op jit(solution)/shard_map/reduce_sum | solution.py:90
  186.3 3.6 %psum.7 = f32[2048]{0:T(1024)S(1)} all-reduce(f32[2048]{0:T(1024)S(1)} %multiply_reduce_fusion), channel_id=1, replica_groups=mesh['seq'=16,'chan'=2] {'chan'}, use_global_device_ids=true, to_apply=%region_9.10 | all-reduce | flops 2048 | bytes 16384 | tf_op jit(solution)/shard_map/psum | solution.py:91
  189.9 7.7 %multiply_convert_fusion.2 = bf16[2048,1024]{0,1:T(8,128)(2,1)} fusion(f32[1024]{0:T(1024)S(1)} %copy-done.10, f32[2048]{0:T(1024)S(1)} %add_rsqrt_fusion, f32[2048,1024]{0,1:T(8,128)} %bitcast.79, bf16[2048,1024]{0,1:T(8,128)(2,1)} %copy.61), kind=kLoop, calls=%fused_computation.23 | loop fusion | flops 18874368 | bytes 16789504 | tf_op jit(solution)/shard_map/convert_element_type | solution.py:93
  197.6 6.4 %copy.62 = bf16[2048,1024]{1,0:T(8,128)(2,1)} copy(bf16[2048,1024]{0,1:T(8,128)(2,1)} %multiply_convert_fusion.2) | data formatting | bytes 8388608 | tf_op jit(solution)/shard_map/convert_element_type | solution.py:93
  (78 shorter events, 4.4 us)
Async XLA Ops:
  6.5 133.8 %all-gather.3.cloned.1.call-start = ((), (), s32[]{:S(2)}) async-start(), calls=%async_computation | async-start | bytes 4456448 | tf_op jit(solution)/shard_map/all_gather | solution.py:26
  30.4 10.4 %copy-start.4 = (bf16[2048,64]{0,1:T(8,128)(2,1)S(1)}, bf16[2048,64]{0,1:T(8,128)(2,1)}, u32[]{:S(2)}) copy-start(bf16[2048,64]{0,1:T(8,128)(2,1)} %param.12) | copy-start | bytes 786436
  46.4 19.3 %copy-start.12 = (u32[32]{0:T(128)S(1)}, u32[32]{0:T(128)}, u32[]{:S(2)}) copy-start(u32[32]{0:T(128)} %constant.43) | copy-start | bytes 388
  46.4 48.5 %copy-start.5 = (bf16[2048,64]{0,1:T(8,128)(2,1)S(1)}, bf16[2048,64]{0,1:T(8,128)(2,1)}, u32[]{:S(2)}) copy-start(bf16[2048,64]{0,1:T(8,128)(2,1)} %param.13) | copy-start | bytes 786436
  46.4 49.3 %copy-start.6 = (f32[16,2048]{1,0:T(8,128)S(1)}, f32[16,2048]{1,0:T(8,128)}, u32[]{:S(2)}) copy-start(f32[16,2048]{1,0:T(8,128)} %param.14) | copy-start | bytes 393220
  147.1 3.7 %copy-start.3 = (f32[8,16,64,64]{3,2,1,0:T(8,128)S(1)}, f32[8,16,64,64]{3,2,1,0:T(8,128)}, u32[]{:S(2)}) copy-start(f32[8,16,64,64]{3,2,1,0:T(8,128)} %get-tuple-element.34) | copy-start | bytes 6291460
  150.8 2.2 %copy-start.2 = (bf16[8,256,16,64]{1,3,2,0:T(8,128)(2,1)S(1)}, bf16[8,256,16,64]{1,3,2,0:T(8,128)(2,1)}, u32[]{:S(2)}) copy-start(bf16[8,256,16,64]{1,3,2,0:T(8,128)(2,1)} %copy.49) | copy-start | bytes 12582916
  150.8 2.2 %copy-start.7 = (f32[8,256,16]{1,2,0:T(8,128)S(1)}, f32[8,256,16]{1,2,0:T(8,128)}, u32[]{:S(2)}) copy-start(f32[8,256,16]{1,2,0:T(8,128)} %copy.50) | copy-start | bytes 393220
  150.8 2.2 %copy-start.8 = (f32[2,8,8,256]{3,2,0,1:T(8,128)S(1)}, f32[2,8,8,256]{3,2,0,1:T(8,128)}, u32[]{:S(2)}) copy-start(f32[2,8,8,256]{3,2,0,1:T(8,128)} %copy.100) | copy-start | bytes 393220
  150.8 2.2 %copy-start.9 = (pred[256,256]{1,0:T(8,128)(4,1)S(1)}, pred[256,256]{1,0:T(8,128)(4,1)}, u32[]{:S(2)}) copy-start(pred[256,256]{1,0:T(8,128)(4,1)} %iota_compare_fusion) | copy-start | bytes 196612
  150.8 2.2 %copy-start.11 = (f32[16]{0:T(128)S(1)}, f32[16]{0:T(128)}, u32[]{:S(2)}) copy-start(f32[16]{0:T(128)} %param.16) | copy-start | bytes 196
  176.2 7.4 %copy-start.1 = (bf16[2048,1024]{0,1:T(8,128)(2,1)S(1)}, bf16[2048,1024]{0,1:T(8,128)(2,1)}, u32[]{:S(2)}) copy-start(bf16[2048,1024]{0,1:T(8,128)(2,1)} %copy.61) | copy-start | bytes 12582916
  180.4 3.2 %copy-start = (f32[128,8,8,256]{3,1,2,0:T(8,128)}, f32[128,8,8,256]{3,1,2,0:T(8,128)S(1)}, u32[]{:S(2)}) copy-start(f32[128,8,8,256]{3,1,2,0:T(8,128)S(1)} %copy.82) | copy-start | bytes 25165828
  180.4 9.5 %copy-start.10 = (f32[1024]{0:T(1024)S(1)}, f32[1024]{0:T(1024)}, u32[]{:S(2)}) copy-start(f32[1024]{0:T(1024)} %param.17) | copy-start | bytes 12292
Sparse Core Ops, SparseCore 0:
  65.8 74.4 all-gather.2
where the time goes:
time: 215 us; the launch traced here: 211 us
  local copies, waits for them, and re-layouts  69.8 us (32%)
  waiting for transfers between devices  36.4 us (17%)
  blocking collectives  31 us (14%)
  matrix products  30.5 us (14%)
  other arithmetic  28.7 us (13%)
  between operations  14.3 us (7%)
    all_gather x1, waiting for transfers between devices, incoming_state(): lax.all_gather(end_flat[None], 'seq', axis=0, tiled=True)  36.4 us
    unnamed x1, blocking collectives  27.4 us
    reshape x2, local copies, waits for them, and re-layouts, per_device(): x_blocks = x_in.reshape(block_count, BLOCK, head_count, head_width)  21.9 us
    unnamed x34, local copies, waits for them, and re-layouts  16.6 us
    dot_general x1, matrix products, per_device(): jnp.einsum('hbts,bshp->bthp', weights, x_blocks, preferred_element_type=j...  13.3 us
    dynamic_slice x16, local copies, waits for them, and re-layouts, per_device(): lax.scan(carry_blocks, jnp.zeros((head_count, head_width, nstate), jnp.fl...  10.2 us
    add x1, local copies, waits for them, and re-layouts, per_device(): output + skip_gain[None, None, :, None] * x_blocks.astype(jnp.float32)  9.87 us
    another operation x2, other arithmetic  9.07 us
  transfers between devices with their start and end apart: 1, of which 1 were waited for; matrix products, arithmetic and copies ran while one was open for 5% of the time, Pallas kernels for 0%

commit v1 on v0

v1 whole, which is shorter than its diff:
```python
import functools

import jax
import jax.numpy as jnp
from jax import lax
from jax.experimental import pallas as pl
from jax.experimental.pallas import tpu as pltpu
from jax.sharding import PartitionSpec as P

BLOCK = 256
SUB = 64
EPSILON = 1e-05
MESH = pl.DeviceIdType.MESH


def dot(a, b, dims):
    return lax.dot_general(a, b, (dims, ((), ())), preferred_element_type=jnp.float32)


def expand(tile, base, head_width, channels):
    lane = lax.broadcasted_iota(jnp.int32, tile.shape, 1)
    pieces = []
    for j in range(channels // 128):
        index = base + (lane + j * 128) // head_width
        pieces.append(jnp.take_along_axis(tile, index, axis=1, mode="promise_in_bounds"))
    return jnp.concatenate(pieces, axis=1)


def decays(log_ref, step_ref, skip_ref, stack, q, spacing):
    heads, tokens = log_ref.shape
    lane = lax.broadcasted_iota(jnp.int32, (heads, tokens), 1)
    pos = lane % SUB
    cum = log_ref[...]
    s = 1
    while s < SUB:
        cum = cum + jnp.where(pos >= s, pltpu.roll(cum, s, 1), 0.0)
        s *= 2
    total = jnp.where(pos == SUB - 1, cum, 0.0)
    s = 1
    while s < SUB:
        total = total + jnp.where(pos < SUB - s, pltpu.roll(total, tokens - s, 1), 0.0)
        s *= 2
    before = jnp.where(lane >= SUB, pltpu.roll(total, SUB, 1), 0.0)
    s = SUB
    while s < tokens:
        before = before + jnp.where(lane >= s, pltpu.roll(before, s, 1), 0.0)
        s *= 2
    mid = 0.5 * total
    stack[...] = jnp.zeros_like(stack)
    stack[0:heads, :] = jnp.exp(mid - cum) * step_ref[...]
    stack[spacing : spacing + heads, :] = jnp.exp(cum - mid)
    stack[2 * spacing : 2 * spacing + heads, :] = jnp.exp(mid)
    stack[3 * spacing : 3 * spacing + heads, :] = jnp.exp(before + mid)
    stack[4 * spacing : 4 * spacing + heads, :] = jnp.broadcast_to(skip_ref[...], (heads, tokens))
    for j in range(tokens // 128):
        q[j * 128 : (j + 1) * 128, :] = jnp.transpose(stack[:, j * 128 : (j + 1) * 128])


def main_kernel(
    n, nchan, spacing,
    x_hbm, gate_hbm, b_ref, c_ref, step_ref, log_ref, skip_ref,
    out_hbm, sq_out,
    x, gate, xs, local, base, es, gated, stack, q, state,
    total_row, totals, give, got, back, entering, sq, sq_got,
    x_sem, gate_sem, out_sem, sems, sq_sems,
):
    tokens, channels = x.shape
    heads = log_ref.shape[0]
    head_width = channels // heads
    nstate = b_ref.shape[1]
    blocks = tokens // BLOCK
    subs = BLOCK // SUB
    rows = nstate // n
    me = lax.axis_index("seq")
    mine = lax.axis_index("chan")

    def block_copy(src, dst, sem, i):
        r = pl.ds(i * BLOCK, BLOCK)
        return pltpu.make_async_copy(src.at[r], dst.at[r], sem.at[i])

    for i in range(blocks):
        block_copy(x_hbm, x, x_sem, i).start()
    for i in range(blocks):
        block_copy(gate_hbm, gate, gate_sem, i).start()

    barrier = pltpu.get_barrier_semaphore()

    @pl.loop(1, n)
    def _(i):
        pl.semaphore_signal(barrier, inc=1, device_id={"seq": lax.rem(me + i, n)}, device_id_type=MESH)

    for i in range(1, nchan):
        pl.semaphore_signal(barrier, inc=1, device_id={"chan": lax.rem(mine + i, nchan)}, device_id_type=MESH)

    def seq_copy(src, dst, kind, to, slot):
        return pltpu.make_async_remote_copy(
            src_ref=src, dst_ref=dst,
            send_sem=sems.at[kind, 0, to], recv_sem=sems.at[kind, 1, slot],
            device_id={"seq": to}, device_id_type=MESH,
        )

    decays(log_ref, step_ref, skip_ref, stack, q, spacing)
    wide = functools.partial(expand, head_width=head_width, channels=channels)
    last = q[tokens - 8 : tokens, :]
    total_row[...] = (wide(last, 2 * spacing) * wide(last, 3 * spacing))[0:1]
    pl.semaphore_wait(barrier, n - 1 + nchan - 1)

    @pl.loop(1, n)
    def _(i):
        to = lax.rem(me + i, n)
        seq_copy(total_row, totals.at[me], 0, to, me).start()

    totals[me] = total_row[...]
    state[...] = jnp.zeros_like(state)

    def times(matrix, row8):
        r, w = matrix.shape
        return (matrix.reshape(r // 8, 8, w) * row8[None]).reshape(r, w)

    @pl.loop(0, blocks)
    def _(i):
        block_copy(x_hbm, x, x_sem, i).wait()
        for j in range(subs):
            start = pl.multiple_of(i * BLOCK + j * SUB, SUB)
            r = pl.ds(start, SUB)
            scaled = (x[r, :].astype(jnp.float32) * wide(q[r, :], 0)).astype(jnp.bfloat16)
            xs[r, :] = scaled
            g = wide(q[pl.ds(start, 8), :], 2 * spacing)
            here = times(state[...], g)
            local[i * subs + j] = here
            state[...] = times(here + dot(b_ref[r, :], scaled, ((0,), (0,))), g)

    for k in range(n):
        give[k] = state[k * rows : (k + 1) * rows, :]

    @pl.loop(1, n)
    def _(i):
        to = lax.rem(me + i, n)
        seq_copy(give.at[to], got.at[me], 1, to, me).start()

    got[me] = give[me]
    skip8 = wide(q[0:8, :], 4 * spacing)
    row = lax.broadcasted_iota(jnp.int32, (SUB, SUB), 0)
    col = lax.broadcasted_iota(jnp.int32, (SUB, SUB), 1)

    def fill(i):
        block_copy(gate_hbm, gate, gate_sem, i).wait()
        for j in range(subs):
            r = pl.ds(pl.multiple_of(i * BLOCK + j * SUB, SUB), SUB)
            scores = dot(c_ref[r, :], b_ref[r, :], ((1,), (1,)))
            scores = jnp.where(row >= col, scores, 0.0).astype(jnp.bfloat16)
            inside = dot(scores, xs[r, :], ((1,), (0,)))
            e2 = wide(q[r, :], spacing)
            half = 0.5 * gate[r, :].astype(jnp.float32)
            silu = half + half * jnp.tanh(half)
            base[r, :] = (e2 * inside + times(x[r, :].astype(jnp.float32), skip8)) * silu
            es[r, :] = e2 * silu

    pl.loop(0, blocks // 2)(fill)

    @pl.loop(1, n)
    def _(i):
        other = lax.rem(me + i, n)
        seq_copy(total_row, totals.at[other], 0, other, other).wait()
        seq_copy(give.at[other], got.at[other], 1, other, other).wait()

    prefix = jnp.zeros((rows, channels), jnp.float32)
    for k in range(n):
        back[k] = prefix
        if k < n - 1:
            prefix = totals[k] * prefix + got[k]

    @pl.loop(1, n)
    def _(i):
        to = lax.rem(me + i, n)
        seq_copy(back.at[to], entering.at[me], 2, to, me).start()

    entering[me] = back[me]
    pl.loop(blocks // 2, blocks)(fill)

    @pl.loop(1, n)
    def _(i):
        other = lax.rem(me + i, n)
        seq_copy(back.at[other], entering.at[other], 2, other, other).wait()

    for k in range(n):
        state[k * rows : (k + 1) * rows, :] = entering[k]

    @pl.loop(0, blocks)
    def _(i):
        sums = []
        for j in range(subs):
            start = pl.multiple_of(i * BLOCK + j * SUB, SUB)
            r = pl.ds(start, SUB)
            g = wide(q[pl.ds(start, 8), :], 3 * spacing)
            here = (local[i * subs + j] + times(state[...], g)).astype(jnp.bfloat16)
            value = base[r, :] + es[r, :] * dot(c_ref[r, :], here, ((1,), (0,)))
            gated[r, :] = value.astype(jnp.bfloat16)
            square = value * value
            part = square[:, 0:128]
            for k in range(1, channels // 128):
                part = part + square[:, k * 128 : (k + 1) * 128]
            sums.append(part)
        for j in range(BLOCK // 128):
            pair = jnp.concatenate(sums[2 * j : 2 * j + 2], axis=0)
            sq[i * (BLOCK // 128) + j] = jnp.sum(jnp.transpose(pair), axis=0, keepdims=True)
        block_copy(gated, out_hbm, out_sem, i).start()

    def chan_copy(to, slot):
        return pltpu.make_async_remote_copy(
            src_ref=sq, dst_ref=sq_got.at[slot],
            send_sem=sq_sems.at[0, to], recv_sem=sq_sems.at[1, slot],
            device_id={"chan": to}, device_id_type=MESH,
        )

    for i in range(1, nchan):
        chan_copy(lax.rem(mine + i, nchan), mine).start()
    sq_got[mine] = sq[...]
    for i in range(blocks):
        block_copy(gated, out_hbm, out_sem, i).wait()
    for i in range(1, nchan):
        other = lax.rem(mine + i, nchan)
        chan_copy(other, other).wait()
    summed = sq_got[0]
    for i in range(1, nchan):
        summed = summed + sq_got[i]
    sq_out[...] = summed


def norm_kernel(total_channels, gated_ref, sq_ref, gain_ref, out_ref):
    channels = gated_ref.shape[1]
    gain = gain_ref[...]
    for j in range(gated_ref.shape[0] // 128):
        factor = lax.rsqrt(sq_ref[j] / total_channels + EPSILON)
        column = jnp.transpose(jnp.broadcast_to(factor, (128, 128)))
        r = slice(j * 128, (j + 1) * 128)
        for k in range(channels // 128):
            w = slice(k * 128, (k + 1) * 128)
            out_ref[r, w] = (gated_ref[r, w].astype(jnp.float32) * column * gain[:, w]).astype(out_ref.dtype)


def per_device(n, nchan, x_in, gate_in, b_in, c_in, step_size, log_keep, skip_gain, norm_gain):
    tokens, channels = x_in.shape
    heads = step_size.shape[0]
    nstate = b_in.shape[1]
    spacing = -(-heads // 8) * 8
    rows = nstate // n
    blocks = tokens // BLOCK
    f32, bf16 = jnp.float32, jnp.bfloat16
    vmem = pl.BlockSpec(memory_space=pltpu.VMEM)
    anywhere = pl.BlockSpec(memory_space=pl.ANY)
    gated, squares = pl.pallas_call(
        functools.partial(main_kernel, n, nchan, spacing),
        out_shape=(
            jax.ShapeDtypeStruct((tokens, channels), bf16),
            jax.ShapeDtypeStruct((tokens // 128, 1, 128), f32),
        ),
        in_specs=[anywhere, anywhere] + [vmem] * 5,
        out_specs=(anywhere, vmem),
        scratch_shapes=[
            pltpu.VMEM((tokens, channels), bf16),
            pltpu.VMEM((tokens, channels), bf16),
            pltpu.VMEM((tokens, channels), bf16),
            pltpu.VMEM((tokens // SUB, nstate, channels), f32),
            pltpu.VMEM((tokens, channels), f32),
            pltpu.VMEM((tokens, channels), f32),
            pltpu.VMEM((tokens, channels), bf16),
            pltpu.VMEM((128, tokens), f32),
            pltpu.VMEM((tokens, 128), f32),
            pltpu.VMEM((nstate, channels), f32),
            pltpu.VMEM((1, channels), f32),
            pltpu.VMEM((n, 1, channels), f32),
            pltpu.VMEM((n, rows, channels), f32),
            pltpu.VMEM((n, rows, channels), f32),
            pltpu.VMEM((n, rows, channels), f32),
            pltpu.VMEM((n, rows, channels), f32),
            pltpu.VMEM((tokens // 128, 1, 128), f32),
            pltpu.VMEM((nchan, tokens // 128, 1, 128), f32),
            pltpu.SemaphoreType.DMA((blocks,)),
            pltpu.SemaphoreType.DMA((blocks,)),
            pltpu.SemaphoreType.DMA((blocks,)),
            pltpu.SemaphoreType.DMA((3, 2, n)),
            pltpu.SemaphoreType.DMA((2, nchan)),
        ],
        compiler_params=pltpu.CompilerParams(
            collective_id=0, has_side_effects=True, vmem_limit_bytes=60 * 2**20
        ),
        name="scan",
    )(x_in, gate_in, b_in, c_in, step_size, log_keep, skip_gain[:, None])
    return pl.pallas_call(
        functools.partial(norm_kernel, channels * nchan),
        grid=(blocks,),
        out_shape=jax.ShapeDtypeStruct((tokens, channels), bf16),
        in_specs=[
            pl.BlockSpec((BLOCK, channels), lambda i: (i, 0)),
            pl.BlockSpec((BLOCK // 128, 1, 128), lambda i: (i, 0, 0)),
            pl.BlockSpec((1, channels), lambda i: (0, 0)),
        ],
        out_specs=pl.BlockSpec((BLOCK, channels), lambda i: (i, 0)),
        compiler_params=pltpu.CompilerParams(dimension_semantics=("arbitrary",)),
        name="norm",
    )(gated, squares, norm_gain[None, :])


def solution(mesh):
    in_specs = (
        P("seq", "chan"),
        P("seq", "chan"),
        P("seq", None),
        P("seq", None),
        P("chan", "seq"),
        P("chan", "seq"),
        P("chan"),
        P("chan"),
    )
    return jax.shard_map(
        functools.partial(per_device, mesh.shape["seq"], mesh.shape["chan"]),
        mesh=mesh,
        in_specs=in_specs,
        out_specs=P("seq", "chan"),
        check_vma=False,
    )
```

time: 215 us -> 46.7 us (0.22); the launches traced: 211 us -> 46.3 us
  local copies, waits for them, and re-layouts: 69.8 us -> 5.23 us
  Pallas kernels: 0 us -> 41.1 us
  waiting for transfers between devices: 36.4 us -> 0 us
  blocking collectives: 31 us -> 0 us
  matrix products: 30.5 us -> 0 us
  other arithmetic: 28.7 us -> 0 us
  between operations: 14.3 us -> 0.01 us
    pallas_call x0 -> x2, Pallas kernels: none -> 41.1 us  [the longest x1 33.8 us: per_device(): pl.pallas_call(functools.partial(main_kernel, n, nchan, spacing), out_sha...]
    all_gather x1 -> x0, waiting for transfers between devices: 36.4 us -> none  [incoming_state(): lax.all_gather(end_flat[None], 'seq', axis=0, tiled=True)]
    dot_general x6 -> x0, matrix products: 30.5 us -> none  [the longest x1 13.3 us: per_device(): jnp.einsum('hbts,bshp->bthp', weights, x_blocks, preferred_element_type=j...]
    unnamed x1 -> x0, blocking collectives: 27.4 us -> none
    reshape x4 -> x0, local copies, waits for them, and re-layouts: 23 us -> none  [the longest x2 21.9 us: per_device(): x_blocks = x_in.reshape(block_count, BLOCK, head_count, head_width)]
    unnamed x34 -> x2, local copies, waits for them, and re-layouts: 16.6 us -> 3.9 us
    dynamic_slice x16 -> x0, local copies, waits for them, and re-layouts: 10.2 us -> none  [per_device(): lax.scan(carry_blocks, jnp.zeros((head_count, head_width, nstate), jnp.fl...]
    add x1 -> x0, local copies, waits for them, and re-layouts: 9.87 us -> none  [per_device(): output + skip_gain[None, None, :, None] * x_blocks.astype(jnp.float32)]
  transfers between devices with their start and end apart: 1 -> 0, of which waited for: 1 -> 0; matrix products, arithmetic and copies ran while one was open for 5% -> 0% of each run, Pallas kernels for 0% -> 0%
where the time goes in v1:
time: 46.7 us; the launch traced here: 46.3 us
  Pallas kernels  41.1 us (88%)
  local copies, waits for them, and re-layouts  5.23 us (11%)
    pallas_call x1, Pallas kernels, per_device(): pl.pallas_call(functools.partial(main_kernel, n, nchan, spacing), out_sha...  33.8 us
    pallas_call x1, Pallas kernels, per_device(): pl.pallas_call(functools.partial(norm_kernel, channels * nchan), grid=(bl...  7.3 us
    unnamed x2, local copies, waits for them, and re-layouts  3.9 us
    broadcast_in_dim x1, local copies, waits for them, and re-layouts, per_device(): skip_gain[:, None]  1.32 us

profile of v1, /device:TPU:25, one launch (start us, length us, event | category | flops | bytes accessed | tf_op | source)
XLA Modules:
  0.0 46.3 jit_solution(13177569387389145420)
XLA Ops:
  0.0 1.3 %copy.11.skip_ref = f32[16,1]{1,0:T(8,128)} copy(f32[16,1]{0,1:T(1,128)} %bitcast.3) | data formatting | bytes 128 | tf_op jit(solution)/shard_map/broadcast_in_dim | solution.py:289
  1.3 2.0 %copy.9.b_ref = bf16[2048,64]{1,0:T(8,128)(2,1)} copy(bf16[2048,64]{0,1:T(8,128)(2,1)} %param.10) | data formatting | bytes 524288 | tf_op args[2]
  3.3 1.9 %copy.10.c_ref = bf16[2048,64]{1,0:T(8,128)(2,1)} copy(bf16[2048,64]{0,1:T(8,128)(2,1)} %param.11) | data formatting | bytes 524288 | tf_op args[3]
  5.2 33.8 %scan.1 = (bf16[2048,1024]{1,0:T(8,128)(2,1)}, f32[16,1,128]{2,1,0:T(1,128)}) custom-call(bf16[2048,1024]{1,0:T(8,128)(2,1)} %x_hbm.1, bf16[2048,1024]{1,0:T(8,128)(2,1)} %gate_hbm.1, bf16[2048,64]{1,0:T(8,128)(2,1)} %copy.9.b_ref, bf16[2048,64]{1,0:T(8,128)(2,1)} %copy.10.c_ref, f32[16,2048]{1,0:T(8,128)} %step_ref.1, f32[16,2048]{1,0:T(8,128)} %log_ref.1, ...), custom_call_target="tpu_custom_call" | custom-call | tf_op jit(solution)/shard_map/scan/pallas_call | solution.py:252
  39.0 7.3 %norm.1 = bf16[2048,1024]{1,0:T(8,128)(2,1)} custom-call(bf16[2048,1024]{1,0:T(8,128)(2,1)} %get-tuple-element.7.gated_ref, f32[16,1,128]{2,1,0:T(1,128)} %get-tuple-element.8.sq_ref, f32[1,1024]{1,0:T(1,128)} %bitcast.2), custom_call_target="tpu_custom_call" | custom-call | tf_op jit(solution)/shard_map/norm/pallas_call | solution.py:290

commit v2 on v1

--- a/solution.py
+++ b/solution.py
@@ -26,7 +26,7 @@
     return jnp.concatenate(pieces, axis=1)
 
 
-def decays(log_ref, step_ref, skip_ref, stack, q, spacing):
+def decays(log_ref, step_ref, stack, q, spacing):
     heads, tokens = log_ref.shape
     lane = lax.broadcasted_iota(jnp.int32, (heads, tokens), 1)
     pos = lane % SUB
@@ -51,7 +51,6 @@
     stack[spacing : spacing + heads, :] = jnp.exp(cum - mid)
     stack[2 * spacing : 2 * spacing + heads, :] = jnp.exp(mid)
     stack[3 * spacing : 3 * spacing + heads, :] = jnp.exp(before + mid)
-    stack[4 * spacing : 4 * spacing + heads, :] = jnp.broadcast_to(skip_ref[...], (heads, tokens))
     for j in range(tokens // 128):
         q[j * 128 : (j + 1) * 128, :] = jnp.transpose(stack[:, j * 128 : (j + 1) * 128])
 
@@ -59,15 +58,15 @@
 def main_kernel(
     n, nchan, spacing,
     x_hbm, gate_hbm, b_ref, c_ref, step_ref, log_ref, skip_ref,
-    out_hbm, sq_out,
-    x, gate, xs, local, base, es, gated, stack, q, state,
+    base, sq_out,
+    x, gate, xs, local, es, c, stack, q, skip_tile, state,
     total_row, totals, give, got, back, entering, sq, sq_got,
-    x_sem, gate_sem, out_sem, sems, sq_sems,
+    x_sem, gate_sem, sems, sq_sems,
 ):
     tokens, channels = x.shape
     heads = log_ref.shape[0]
     head_width = channels // heads
-    nstate = b_ref.shape[1]
+    nstate = b_ref.shape[0]
     blocks = tokens // BLOCK
     subs = BLOCK // SUB
     rows = nstate // n
@@ -99,7 +98,12 @@
             device_id={"seq": to}, device_id_type=MESH,
         )
 
-    decays(log_ref, step_ref, skip_ref, stack, q, spacing)
+    decays(log_ref, step_ref, stack, q, spacing)
+    skip_tile[...] = jnp.zeros_like(skip_tile)
+    skip_tile[:, 0:heads] = jnp.broadcast_to(skip_ref[...], (8, heads))
+    for j in range(tokens // 128):
+        w = slice(j * 128, (j + 1) * 128)
+        c[w, :] = jnp.transpose(c_ref[:, w].astype(jnp.float32)).astype(jnp.bfloat16)
     wide = functools.partial(expand, head_width=head_width, channels=channels)
     last = q[tokens - 8 : tokens, :]
     total_row[...] = (wide(last, 2 * spacing) * wide(last, 3 * spacing))[0:1]
@@ -112,6 +116,10 @@
 
     totals[me] = total_row[...]
     state[...] = jnp.zeros_like(state)
+
+    def b_sub(i, j):
+        pair = b_ref[:, pl.ds(pl.multiple_of(i * BLOCK + j // 2 * 128, 128), 128)]
+        return pair[:, j % 2 * SUB : (j % 2 + 1) * SUB]
 
     def times(matrix, row8):
         r, w = matrix.shape
@@ -128,7 +136,7 @@
             g = wide(q[pl.ds(start, 8), :], 2 * spacing)
             here = times(state[...], g)
             local[i * subs + j] = here
-            state[...] = times(here + dot(b_ref[r, :], scaled, ((0,), (0,))), g)
+            state[...] = times(here + dot(b_sub(i, j), scaled, ((1,), (0,))), g)
 
     for k in range(n):
         give[k] = state[k * rows : (k + 1) * rows, :]
@@ -139,7 +147,7 @@
         seq_copy(give.at[to], got.at[me], 1, to, me).start()
 
     got[me] = give[me]
-    skip8 = wide(q[0:8, :], 4 * spacing)
+    skip8 = wide(skip_tile[...], 0)
     row = lax.broadcasted_iota(jnp.int32, (SUB, SUB), 0)
     col = lax.broadcasted_iota(jnp.int32, (SUB, SUB), 1)
 
@@ -147,7 +155,7 @@
         block_copy(gate_hbm, gate, gate_sem, i).wait()
         for j in range(subs):
             r = pl.ds(pl.multiple_of(i * BLOCK + j * SUB, SUB), SUB)
-            scores = dot(c_ref[r, :], b_ref[r, :], ((1,), (1,)))
+            scores = dot(c[r, :], b_sub(i, j), ((1,), (0,)))
             scores = jnp.where(row >= col, scores, 0.0).astype(jnp.bfloat16)
             inside = dot(scores, xs[r, :], ((1,), (0,)))
             e2 = wide(q[r, :], spacing)
@@ -194,8 +202,8 @@
             r = pl.ds(start, SUB)
             g = wide(q[pl.ds(start, 8), :], 3 * spacing)
             here = (local[i * subs + j] + times(state[...], g)).astype(jnp.bfloat16)
-            value = base[r, :] + es[r, :] * dot(c_ref[r, :], here, ((1,), (0,)))
-            gated[r, :] = value.astype(jnp.bfloat16)
+            value = base[r, :] + es[r, :] * dot(c[r, :], here, ((1,), (0,)))
+            base[r, :] = value
             square = value * value
             part = square[:, 0:128]
             for k in range(1, channels // 128):
@@ -204,7 +212,6 @@
         for j in range(BLOCK // 128):
             pair = jnp.concatenate(sums[2 * j : 2 * j + 2], axis=0)
             sq[i * (BLOCK // 128) + j] = jnp.sum(jnp.transpose(pair), axis=0, keepdims=True)
-        block_copy(gated, out_hbm, out_sem, i).start()
 
     def chan_copy(to, slot):
         return pltpu.make_async_remote_copy(
@@ -216,8 +223,6 @@
     for i in range(1, nchan):
         chan_copy(lax.rem(mine + i, nchan), mine).start()
     sq_got[mine] = sq[...]
-    for i in range(blocks):
-        block_copy(gated, out_hbm, out_sem, i).wait()
     for i in range(1, nchan):
         other = lax.rem(mine + i, nchan)
         chan_copy(other, other).wait()
@@ -227,16 +232,27 @@
     sq_out[...] = summed
 
 
-def norm_kernel(total_channels, gated_ref, sq_ref, gain_ref, out_ref):
-    channels = gated_ref.shape[1]
-    gain = gain_ref[...]
-    for j in range(gated_ref.shape[0] // 128):
-        factor = lax.rsqrt(sq_ref[j] / total_channels + EPSILON)
-        column = jnp.transpose(jnp.broadcast_to(factor, (128, 128)))
-        r = slice(j * 128, (j + 1) * 128)
-        for k in range(channels // 128):
-            w = slice(k * 128, (k + 1) * 128)
-            out_ref[r, w] = (gated_ref[r, w].astype(jnp.float32) * column * gain[:, w]).astype(out_ref.dtype)
+def norm_kernel(total_channels, gated, sq_ref, gain_ref, out_hbm, out, sem):
+    tokens, channels = gated.shape
+
+    def copy(i):
+        r = pl.ds(i * BLOCK, BLOCK)
+        return pltpu.make_async_copy(out.at[r], out_hbm.at[r], sem.at[i])
+
+    @pl.loop(0, tokens // BLOCK)
+    def _(i):
+        gain = gain_ref[...]
+        for j in range(BLOCK // 128):
+            factor = lax.rsqrt(sq_ref[i * (BLOCK // 128) + j] / total_channels + EPSILON)
+            column = jnp.transpose(jnp.broadcast_to(factor, (128, 128)))
+            r = pl.ds(pl.multiple_of(i * BLOCK + j * 128, 128), 128)
+            for k in range(channels // 128):
+                w = slice(k * 128, (k + 1) * 128)
+                out[r, w] = (gated[r, w] * column * gain[:, w]).astype(out.dtype)
+        copy(i).start()
+
+    for i in range(tokens // BLOCK):
+        copy(i).wait()
 
 
 def per_device(n, nchan, x_in, gate_in, b_in, c_in, step_size, log_keep, skip_gain, norm_gain):
@@ -248,25 +264,25 @@
     blocks = tokens // BLOCK
     f32, bf16 = jnp.float32, jnp.bfloat16
     vmem = pl.BlockSpec(memory_space=pltpu.VMEM)
-    anywhere = pl.BlockSpec(memory_space=pl.ANY)
+    anywhere = pl.BlockSpec(memory_space=pltpu.HBM)
     gated, squares = pl.pallas_call(
         functools.partial(main_kernel, n, nchan, spacing),
         out_shape=(
-            jax.ShapeDtypeStruct((tokens, channels), bf16),
+            pltpu.VMEM((tokens, channels), f32),
             jax.ShapeDtypeStruct((tokens // 128, 1, 128), f32),
         ),
         in_specs=[anywhere, anywhere] + [vmem] * 5,
-        out_specs=(anywhere, vmem),
+        out_specs=(vmem, vmem),
         scratch_shapes=[
             pltpu.VMEM((tokens, channels), bf16),
             pltpu.VMEM((tokens, channels), bf16),
             pltpu.VMEM((tokens, channels), bf16),
             pltpu.VMEM((tokens // SUB, nstate, channels), f32),
             pltpu.VMEM((tokens, channels), f32),
-            pltpu.VMEM((tokens, channels), f32),
-            pltpu.VMEM((tokens, channels), bf16),
+            pltpu.VMEM((tokens, nstate), bf16),
             pltpu.VMEM((128, tokens), f32),
             pltpu.VMEM((tokens, 128), f32),
+            pltpu.VMEM((8, 128), f32),
             pltpu.VMEM((nstate, channels), f32),
             pltpu.VMEM((1, channels), f32),
             pltpu.VMEM((n, 1, channels), f32),
@@ -278,26 +294,21 @@
             pltpu.VMEM((nchan, tokens // 128, 1, 128), f32),
             pltpu.SemaphoreType.DMA((blocks,)),
             pltpu.SemaphoreType.DMA((blocks,)),
-            pltpu.SemaphoreType.DMA((blocks,)),
             pltpu.SemaphoreType.DMA((3, 2, n)),
             pltpu.SemaphoreType.DMA((2, nchan)),
         ],
         compiler_params=pltpu.CompilerParams(
-            collective_id=0, has_side_effects=True, vmem_limit_bytes=60 * 2**20
+            collective_id=0, has_side_effects=True, vmem_limit_bytes=50 * 2**20
         ),
         name="scan",
-    )(x_in, gate_in, b_in, c_in, step_size, log_keep, skip_gain[:, None])
+    )(x_in, gate_in, b_in.T, c_in.T, step_size, log_keep, skip_gain[None, :])
     return pl.pallas_call(
         functools.partial(norm_kernel, channels * nchan),
-        grid=(blocks,),
         out_shape=jax.ShapeDtypeStruct((tokens, channels), bf16),
-        in_specs=[
-            pl.BlockSpec((BLOCK, channels), lambda i: (i, 0)),
-            pl.BlockSpec((BLOCK // 128, 1, 128), lambda i: (i, 0, 0)),
-            pl.BlockSpec((1, channels), lambda i: (0, 0)),
-        ],
-        out_specs=pl.BlockSpec((BLOCK, channels), lambda i: (i, 0)),
-        compiler_params=pltpu.CompilerParams(dimension_semantics=("arbitrary",)),
+        in_specs=[vmem] * 3,
+        out_specs=anywhere,
+        scratch_shapes=[pltpu.VMEM((tokens, channels), bf16), pltpu.SemaphoreType.DMA((blocks,))],
+        compiler_params=pltpu.CompilerParams(vmem_limit_bytes=16 * 2**20),
         name="norm",
     )(gated, squares, norm_gain[None, :])
 

time: 46.7 us -> 37.3 us (0.80)
  Pallas kernels: 41.1 us -> 36.3 us
  local copies, waits for them, and re-layouts: 5.23 us -> 0.69 us
    pallas_call x1, Pallas kernels: 7.3 us -> 2.67 us  [per_device(): pl.pallas_call(functools.partial(norm_kernel, channels * nchan), out_shap...]
    unnamed x2 -> x4, local copies, waits for them, and re-layouts: 3.9 us -> 0.69 us
    broadcast_in_dim x1 -> x0, local copies, waits for them, and re-layouts: 1.32 us -> none  [per_device(): skip_gain[:, None]]
where the time goes in v2:
time: 37.3 us; the launch traced here: 37.1 us
  Pallas kernels  36.3 us (97%)
  local copies, waits for them, and re-layouts  0.69 us (2%)
    pallas_call x1, Pallas kernels, per_device(): pl.pallas_call(functools.partial(main_kernel, n, nchan, spacing), out_sha...  33.7 us
    pallas_call x1, Pallas kernels, per_device(): pl.pallas_call(functools.partial(norm_kernel, channels * nchan), out_shap...  2.67 us

profile of v2, /device:TPU:25, one launch (start us, length us, event | category | flops | bytes accessed | tf_op | source)
XLA Modules:
  0.0 37.1 jit_solution(14450226578621119591)
XLA Ops:
  0.0 0.0 copy-start.1
  0.0 33.7 %scan.1 = (f32[2048,1024]{1,0:T(8,128)S(1)}, f32[16,1,128]{2,1,0:T(1,128)}) custom-call(bf16[2048,1024]{1,0:T(8,128)(2,1)} %x_hbm.1, bf16[2048,1024]{1,0:T(8,128)(2,1)} %gate_hbm.1, bf16[64,2048]{1,0:T(8,128)(2,1)} %bitcast.5, bf16[64,2048]{1,0:T(8,128)(2,1)} %bitcast.6, f32[16,2048]{1,0:T(8,128)} %step_ref.1, f32[16,2048]{1,0:T(8,128)} %log_ref.1, ...), custom_call_target="tpu_custom_call" | custom-call | tf_op jit(solution)/shard_map/scan/pallas_call | solution.py:268
  33.7 0.0 copy-done.1
  33.7 0.0 copy-start
  33.7 0.7 %copy-done = f32[16,1,128]{2,1,0:T(1,128)S(1)} copy-done((f32[16,1,128]{2,1,0:T(1,128)S(1)}, f32[16,1,128]{2,1,0:T(1,128)}, u32[]{:S(2)}) %copy-start) | copy-done | bytes 8216
  34.4 2.7 %norm.1 = bf16[2048,1024]{1,0:T(8,128)(2,1)} custom-call(f32[2048,1024]{1,0:T(8,128)S(1)} %get-tuple-element.7.gated, f32[16,1,128]{2,1,0:T(1,128)S(1)} %copy-done, f32[1,1024]{1,0:T(1,128)S(1)} %bitcast.4), custom_call_target="tpu_custom_call" | custom-call | tf_op jit(solution)/shard_map/norm/pallas_call | solution.py:305
Async XLA Ops:
  0.0 33.7 %copy-start.1 = (f32[1024]{0:T(1024)S(1)}, f32[1024]{0:T(1024)}, u32[]{:S(2)}) copy-start(f32[1024]{0:T(1024)} %param.15) | copy-start | bytes 12292
  33.7 0.7 %copy-start = (f32[16,1,128]{2,1,0:T(1,128)S(1)}, f32[16,1,128]{2,1,0:T(1,128)}, u32[]{:S(2)}) copy-start(f32[16,1,128]{2,1,0:T(1,128)} %get-tuple-element.8.sq_ref) | copy-start | bytes 24580

commit v3 on v2

--- a/solution.py
+++ b/solution.py
@@ -60,8 +60,8 @@
     x_hbm, gate_hbm, b_ref, c_ref, step_ref, log_ref, skip_ref,
     base, sq_out,
     x, gate, xs, local, es, c, stack, q, skip_tile, state,
-    total_row, totals, give, got, back, entering, sq, sq_got,
-    x_sem, gate_sem, sems, sq_sems,
+    total_row, totals, give, got, back, entering, low_total, low_got, sq, sq_got,
+    x_sem, gate_sem, sems, hop_sems, sq_sems,
 ):
     tokens, channels = x.shape
     heads = log_ref.shape[0]
@@ -69,7 +69,7 @@
     nstate = b_ref.shape[0]
     blocks = tokens // BLOCK
     subs = BLOCK // SUB
-    rows = nstate // n
+    rows = nstate // (n // 2)
     me = lax.axis_index("seq")
     mine = lax.axis_index("chan")
 
@@ -82,19 +82,30 @@
     for i in range(blocks):
         block_copy(gate_hbm, gate, gate_sem, i).start()
 
+    group = n // 2
+    half, place = me // group, lax.rem(me, group)
+    across = lax.rem(me + group, n)
+
+    def peer(i):
+        slot = lax.rem(place + i, group)
+        return slot, half * group + slot
+
     barrier = pltpu.get_barrier_semaphore()
 
-    @pl.loop(1, n)
-    def _(i):
-        pl.semaphore_signal(barrier, inc=1, device_id={"seq": lax.rem(me + i, n)}, device_id_type=MESH)
+    @pl.loop(1, group)
+    def _(i):
+        pl.semaphore_signal(barrier, inc=1, device_id={"seq": peer(i)[1]}, device_id_type=MESH)
+
+    pl.semaphore_signal(barrier, inc=1, device_id={"seq": across}, device_id_type=MESH)
 
     for i in range(1, nchan):
         pl.semaphore_signal(barrier, inc=1, device_id={"chan": lax.rem(mine + i, nchan)}, device_id_type=MESH)
 
-    def seq_copy(src, dst, kind, to, slot):
+    def seq_copy(src, dst, kind, i, slot):
+        give_slot, to = peer(i)
         return pltpu.make_async_remote_copy(
             src_ref=src, dst_ref=dst,
-            send_sem=sems.at[kind, 0, to], recv_sem=sems.at[kind, 1, slot],
+            send_sem=sems.at[kind, 0, give_slot], recv_sem=sems.at[kind, 1, slot],
             device_id={"seq": to}, device_id_type=MESH,
         )
 
@@ -107,14 +118,6 @@
     wide = functools.partial(expand, head_width=head_width, channels=channels)
     last = q[tokens - 8 : tokens, :]
     total_row[...] = (wide(last, 2 * spacing) * wide(last, 3 * spacing))[0:1]
-    pl.semaphore_wait(barrier, n - 1 + nchan - 1)
-
-    @pl.loop(1, n)
-    def _(i):
-        to = lax.rem(me + i, n)
-        seq_copy(total_row, totals.at[me], 0, to, me).start()
-
-    totals[me] = total_row[...]
     state[...] = jnp.zeros_like(state)
 
     def b_sub(i, j):
@@ -138,15 +141,17 @@
             local[i * subs + j] = here
             state[...] = times(here + dot(b_sub(i, j), scaled, ((1,), (0,))), g)
 
-    for k in range(n):
+    for k in range(group):
         give[k] = state[k * rows : (k + 1) * rows, :]
-
-    @pl.loop(1, n)
-    def _(i):
-        to = lax.rem(me + i, n)
-        seq_copy(give.at[to], got.at[me], 1, to, me).start()
-
-    got[me] = give[me]
+    pl.semaphore_wait(barrier, group + nchan - 1)
+
+    @pl.loop(1, group)
+    def _(i):
+        seq_copy(give.at[peer(i)[0]], got.at[place], 1, i, place).start()
+        seq_copy(total_row, totals.at[place], 0, i, place).start()
+
+    got[place] = give[place]
+    totals[place] = total_row[...]
     skip8 = wide(skip_tile[...], 0)
     row = lax.broadcasted_iota(jnp.int32, (SUB, SUB), 0)
     col = lax.broadcasted_iota(jnp.int32, (SUB, SUB), 1)
@@ -164,34 +169,59 @@
             base[r, :] = (e2 * inside + times(x[r, :].astype(jnp.float32), skip8)) * silu
             es[r, :] = e2 * silu
 
-    pl.loop(0, blocks // 2)(fill)
-
-    @pl.loop(1, n)
-    def _(i):
-        other = lax.rem(me + i, n)
-        seq_copy(total_row, totals.at[other], 0, other, other).wait()
-        seq_copy(give.at[other], got.at[other], 1, other, other).wait()
-
-    prefix = jnp.zeros((rows, channels), jnp.float32)
-    for k in range(n):
-        back[k] = prefix
-        if k < n - 1:
+    first, second = blocks * 4 // 8, blocks * 5 // 8
+    pl.loop(0, first)(fill)
+
+    @pl.loop(1, group)
+    def _(i):
+        slot = peer(i)[0]
+        seq_copy(give.at[slot], got.at[slot], 1, i, slot).wait()
+        seq_copy(total_row, totals.at[slot], 0, i, slot).wait()
+
+    hop = pltpu.make_async_remote_copy(
+        src_ref=low_total, dst_ref=low_got, send_sem=hop_sems.at[0], recv_sem=hop_sems.at[1],
+        device_id={"seq": across}, device_id_type=MESH,
+    )
+
+    def run(prefix):
+        for k in range(group):
+            back[k] = prefix
             prefix = totals[k] * prefix + got[k]
-
-    @pl.loop(1, n)
-    def _(i):
-        to = lax.rem(me + i, n)
-        seq_copy(back.at[to], entering.at[me], 2, to, me).start()
-
-    entering[me] = back[me]
-    pl.loop(blocks // 2, blocks)(fill)
-
-    @pl.loop(1, n)
-    def _(i):
-        other = lax.rem(me + i, n)
-        seq_copy(back.at[other], entering.at[other], 2, other, other).wait()
-
-    for k in range(n):
+        return prefix
+
+    def send_back():
+        @pl.loop(1, group)
+        def _(i):
+            seq_copy(back.at[peer(i)[0]], entering.at[place], 2, i, place).start()
+
+        entering[place] = back[place]
+
+    @pl.when(half == 0)
+    def _():
+        low_total[...] = run(jnp.zeros((rows, channels), jnp.float32))
+        hop.start()
+        send_back()
+
+    pl.loop(first, second)(fill)
+
+    @pl.when(half == 1)
+    def _():
+        hop.wait_recv()
+        run(low_got[...])
+        send_back()
+
+    pl.loop(second, blocks)(fill)
+
+    @pl.loop(1, group)
+    def _(i):
+        slot = peer(i)[0]
+        seq_copy(back.at[slot], entering.at[slot], 2, i, slot).wait()
+
+    @pl.when(half == 0)
+    def _():
+        hop.wait_send()
+
+    for k in range(group):
         state[k * rows : (k + 1) * rows, :] = entering[k]
 
     @pl.loop(0, blocks)
@@ -260,7 +290,8 @@
     heads = step_size.shape[0]
     nstate = b_in.shape[1]
     spacing = -(-heads // 8) * 8
-    rows = nstate // n
+    group = n // 2
+    rows = nstate // group
     blocks = tokens // BLOCK
     f32, bf16 = jnp.float32, jnp.bfloat16
     vmem = pl.BlockSpec(memory_space=pltpu.VMEM)
@@ -269,7 +300,7 @@
         functools.partial(main_kernel, n, nchan, spacing),
         out_shape=(
             pltpu.VMEM((tokens, channels), f32),
-            jax.ShapeDtypeStruct((tokens // 128, 1, 128), f32),
+            pltpu.VMEM((tokens // 128, 1, 128), f32),
         ),
         in_specs=[anywhere, anywhere] + [vmem] * 5,
         out_specs=(vmem, vmem),
@@ -285,16 +316,19 @@
             pltpu.VMEM((8, 128), f32),
             pltpu.VMEM((nstate, channels), f32),
             pltpu.VMEM((1, channels), f32),
-            pltpu.VMEM((n, 1, channels), f32),
-            pltpu.VMEM((n, rows, channels), f32),
-            pltpu.VMEM((n, rows, channels), f32),
-            pltpu.VMEM((n, rows, channels), f32),
-            pltpu.VMEM((n, rows, channels), f32),
+            pltpu.VMEM((group, 1, channels), f32),
+            pltpu.VMEM((group, rows, channels), f32),
+            pltpu.VMEM((group, rows, channels), f32),
+            pltpu.VMEM((group, rows, channels), f32),
+            pltpu.VMEM((group, rows, channels), f32),
+            pltpu.VMEM((rows, channels), f32),
+            pltpu.VMEM((rows, channels), f32),
             pltpu.VMEM((tokens // 128, 1, 128), f32),
             pltpu.VMEM((nchan, tokens // 128, 1, 128), f32),
             pltpu.SemaphoreType.DMA((blocks,)),
             pltpu.SemaphoreType.DMA((blocks,)),
-            pltpu.SemaphoreType.DMA((3, 2, n)),
+            pltpu.SemaphoreType.DMA((3, 2, group)),
+            pltpu.SemaphoreType.DMA((2,)),
             pltpu.SemaphoreType.DMA((2, nchan)),
         ],
         compiler_params=pltpu.CompilerParams(

time: 37.3 us -> 31.2 us (0.84)
  the two profiles are of different devices: /device:TPU:25 before, /device:TPU:21 now
where the time goes in v3:
time: 31.2 us; the launch traced here: 31.1 us
  Pallas kernels  31 us (99%)
    pallas_call x1, Pallas kernels, per_device(): pl.pallas_call(functools.partial(main_kernel, n, nchan, spacing), out_sha...  28.4 us
    pallas_call x1, Pallas kernels, per_device(): pl.pallas_call(functools.partial(norm_kernel, channels * nchan), out_shap...  2.68 us

profile of v3, /device:TPU:21, one launch (start us, length us, event | category | flops | bytes accessed | tf_op | source)
XLA Modules:
  0.0 31.1 jit_solution(12097390467072322513)
XLA Ops:
  0.0 0.0 copy-start
  0.0 28.4 %scan.1 = (f32[2048,1024]{1,0:T(8,128)S(1)}, f32[16,1,128]{2,1,0:T(1,128)S(1)}) custom-call(bf16[2048,1024]{1,0:T(8,128)(2,1)} %x_hbm.1, bf16[2048,1024]{1,0:T(8,128)(2,1)} %gate_hbm.1, bf16[64,2048]{1,0:T(8,128)(2,1)} %bitcast.5, bf16[64,2048]{1,0:T(8,128)(2,1)} %bitcast.6, f32[16,2048]{1,0:T(8,128)} %step_ref.1, f32[16,2048]{1,0:T(8,128)} %log_ref.1, ...), custom_call_target="tpu_custom_call" | custom-call | tf_op jit(solution)/shard_map/scan/pallas_call | solution.py:299
  28.4 0.0 copy-done
  28.4 2.7 %norm.1 = bf16[2048,1024]{1,0:T(8,128)(2,1)} custom-call(f32[2048,1024]{1,0:T(8,128)S(1)} %get-tuple-element.7.gated, f32[16,1,128]{2,1,0:T(1,128)S(1)} %get-tuple-element.8.sq_ref, f32[1,1024]{1,0:T(1,128)S(1)} %bitcast.4), custom_call_target="tpu_custom_call" | custom-call | tf_op jit(solution)/shard_map/norm/pallas_call | solution.py:339
Async XLA Ops:
  0.0 28.4 %copy-start = (f32[1024]{0:T(1024)S(1)}, f32[1024]{0:T(1024)}, u32[]{:S(2)}) copy-start(f32[1024]{0:T(1024)} %param.15) | copy-start | bytes 12292
